TPU v7x, 32 devices: a whole 2x2x4 slice. The times are simulated.
32 devices in a mesh: fsdp: 4 (over y, core), ctx: 8 (over z, x).
Axes of the slice: x: 2, y: 2, z: 4, core: 2. Of those that a mesh axis runs over, the one named last changes fastest.
Arguments:
- inputs: bfloat16 [4, 4096, 1536], P('fsdp', 'ctx'), may hold values from -8 to 8
- segment_ids: int32 [4, 4096], P('fsdp', 'ctx'), may hold values from 0 to 3, never falling along the last dimension, each value on 1 to 2048 neighbouring positions
- out_grad: bfloat16 [4, 4096, 1536], P('fsdp', 'ctx'), may hold values from -6 to 6
- in_matrix: bfloat16 [1536, 6448], P('fsdp'), may hold values from -0.15625 to 0.15625
- out_matrix: bfloat16 [3072, 1536], P('fsdp'), may hold values from -0.109375 to 0.109375
- conv_taps: bfloat16 [3328, 4], P('fsdp'), may hold values from -3 to 3
- conv_bias: bfloat16 [3328], P('fsdp'), may hold values from -2.5 to 2.5
- dt_bias: bfloat16 [48], P('fsdp'), may hold values from -6 to -2
- decay_log: bfloat16 [48], P('fsdp'), may hold values from -7 to 2.5
- skip_scale: bfloat16 [48], P('fsdp'), may hold values from 0.5 to 2
- mixer_gain: bfloat16 [3072], P('fsdp'), may hold values from 0.5 to 1.5
- input_gain: bfloat16 [1536], P('fsdp'), may hold values from 0.5 to 1.5
Outputs:
- block_out: bfloat16 [4, 4096, 1536], P('fsdp', 'ctx')
- input_grad: bfloat16 [4, 4096, 1536], P('fsdp', 'ctx')
- in_matrix_grad: float32 [1536, 6448], P('fsdp')
- out_matrix_grad: float32 [3072, 1536], P('fsdp')
- conv_taps_grad: float32 [3328, 4], P('fsdp')
- conv_bias_grad: float32 [3328], P('fsdp')
- dt_bias_grad: float32 [48], P('fsdp')
- decay_log_grad: float32 [48], P('fsdp')
- skip_scale_grad: float32 [48], P('fsdp')
- mixer_gain_grad: float32 [3072], P('fsdp')
- input_gain_grad: float32 [1536], P('fsdp')
- rms_stats: float32 [2], replicated
Inputs may be any that keep to these rules, and one draw needn't show every extreme that they name: `segment_ids`: along each sequence the numbers never fall; a run of equal numbers is one document; every number of 0 to 3 is used, and the longest document has exactly 2048 tokens.
All inputs are finite; a program needn't handle non-finite values.
Results may differ from a plain program's by a relative error of at most 0.015.
Values may be sent and summed in bfloat16 or wider, within the bound.
A program may use at most 320 MiB of HBM per device.

v0:
```python
import jax
import jax.numpy as jnp
from jax import lax
from jax.sharding import PartitionSpec as P

D = 1536
HEADS = 48
HDIM = 64
STATE = 128
CONV = 4
GROUP = 256
INNER = 3072
XBC = 3328
epsilon = 1e-05
precise = lax.Precision.HIGHEST


def passed_along(block, axis, distance):
    devices = range(lax.axis_size(axis))
    route = [(i - distance, i) for i in devices if i - distance in devices]
    return lax.ppermute(block, axis, route)


def prefix(x, axis, join, neutral):
    place = lax.axis_index(axis)
    gathered = jax.tree.map(
        lambda a, kind: lax.all_gather(a.astype(kind), axis), x, (jnp.bfloat16, jnp.bfloat16)
    )
    state = jax.tree.map(lambda a, e: jnp.zeros_like(a) + jnp.asarray(e, a.dtype), x, neutral)

    def one(lap, state):
        return join(
            state,
            jax.tree.map(
                lambda a, own: lax.dynamic_index_in_dim(a, lap, 0, False).astype(own.dtype),
                gathered,
                x,
            ),
        )

    return lax.fori_loop(0, place, one, state)


def prefix_2(x, axis, combine, identity):
    count, mine = (lax.axis_size(axis), lax.axis_index(axis))
    everything = jax.tree.map(
        lambda part, kind: lax.all_gather(part.astype(kind), axis),
        x,
        jax.tree.map(lambda a: jnp.bfloat16 if a.dtype == jnp.float32 else a.dtype, x),
    )
    start = jax.tree.map(
        lambda part, zero: jnp.broadcast_to(jnp.asarray(zero, part.dtype), part.shape), x, identity
    )

    def lap(k, before):
        at = count - 1 - k
        reached = at > mine
        new = combine(
            before, jax.tree.map(lambda part, own: part[at].astype(own.dtype), everything, x)
        )
        return jax.tree.map(lambda a, b: jnp.where(reached, a, b), new, before)

    return lax.fori_loop(0, count, lap, start)


def combine(earlier, later_pair):
    return (earlier[0] * later_pair[0], later_pair[0][:, None, None] * earlier[1] + later_pair[1])


def block_step(carry_pair, sliced):
    carried, seg_before, offset = carry_pair
    xblock, bblock, cblock, dblock, lblock, sblock = sliced
    block_len = sblock.shape[0]
    running = jnp.cumsum(lblock, axis=0)
    rowpos = lax.broadcasted_iota(jnp.int32, (block_len, block_len), 0)
    colpos = lax.broadcasted_iota(jnp.int32, (block_len, block_len), 1)
    allowed = (sblock[:, None] == sblock[None, :]) & (colpos <= rowpos)
    log_gap = running.T[:, :, None] - running.T[:, None, :]
    decays = jnp.exp(jnp.where(allowed[None], log_gap, -1e30))
    scores = jnp.dot(cblock, bblock.T, precision=precise)
    mixing = decays * scores[None] * dblock.T[:, None, :]
    y_diag = jnp.einsum("hts,shp->thp", mixing, xblock, precision=precise)
    carry_in = (sblock == seg_before).astype(jnp.float32)
    y_off = (jnp.exp(running) * carry_in[:, None])[:, :, None] * jnp.einsum(
        "tn,hpn->thp", cblock, carried, precision=precise
    )
    final_log = running[block_len - 1]
    tail_weight = (
        jnp.exp(final_log[None, :] - running)
        * (sblock == sblock[block_len - 1]).astype(jnp.float32)[:, None]
        * dblock
    )
    retain = jnp.exp(final_log) * (sblock[block_len - 1] == seg_before).astype(jnp.float32)
    carried = retain[:, None, None] * carried + jnp.einsum(
        "sh,shp,sn->hpn", tail_weight, xblock, bblock, precision=precise
    )
    return (
        (carried, sblock[block_len - 1], offset + final_log),
        (y_diag + y_off, running + offset[None, :]),
    )


def scan_ssd(values, b_rows, c_rows, dt_rows, log_decay, seg_ids, seg_start):
    length = seg_ids.shape[0]
    blocks = length // GROUP
    sliced = (
        values.reshape(blocks, GROUP, HEADS, HDIM),
        b_rows.reshape(blocks, GROUP, STATE),
        c_rows.reshape(blocks, GROUP, STATE),
        dt_rows.reshape(blocks, GROUP, HEADS),
        log_decay.reshape(blocks, GROUP, HEADS),
        seg_ids.reshape(blocks, GROUP),
    )
    initial = (
        jnp.zeros((HEADS, HDIM, STATE), jnp.float32),
        seg_start,
        jnp.zeros((HEADS,), jnp.float32),
    )
    finish, (outputs, running) = lax.scan(jax.checkpoint(block_step), initial, sliced)
    return (outputs.reshape(length, HEADS, HDIM), running.reshape(length, HEADS), finish[0])


def mixer_front(
    ext_rows, dt_raw, conv_taps, conv_bias, dt_bias, decay_log, seg_ext, seg_ids, seg_start
):
    length = seg_ids.shape[0]
    summed = jnp.broadcast_to(conv_bias, (length, conv_bias.shape[0]))
    for tap_index in range(CONV):
        same_doc = (seg_ext[tap_index : tap_index + length] == seg_ids).astype(jnp.float32)
        summed = (
            summed
            + conv_taps[:, tap_index] * ext_rows[tap_index : tap_index + length] * same_doc[:, None]
        )
    active = jax.nn.silu(summed)
    values = active[:, :INNER].reshape(length, HEADS, HDIM)
    b_rows = active[:, INNER : INNER + STATE]
    c_rows = active[:, INNER + STATE :]
    dt_rows = jax.nn.softplus(dt_raw + dt_bias)
    log_decay = -dt_rows * jnp.exp(decay_log)
    y_local, running, carried = scan_ssd(
        values, b_rows, c_rows, dt_rows, log_decay, seg_ids, seg_start
    )
    retain = jnp.exp(running[length - 1]) * (seg_ids[length - 1] == seg_start).astype(jnp.float32)
    return (values, c_rows, running, y_local, carried, retain)


def mixer_tail(
    values, c_rows, running, y_local, carried_in, gate_part, skip_scale, mixer_gain, carry_flag
):
    length = gate_part.shape[0]
    incoming = jnp.einsum("tn,hpn->thp", c_rows, carried_in, precision=precise)
    weights = jnp.exp(running) * carry_flag[:, None]
    mixed_ssd = y_local + weights[:, :, None] * incoming + skip_scale[None, :, None] * values
    gated = mixed_ssd.reshape(length, INNER) * jax.nn.silu(gate_part)
    return gated * lax.rsqrt(jnp.mean(gated * gated, axis=-1, keepdims=True) + epsilon) * mixer_gain


def on_device(
    inputs,
    segment_ids,
    out_grad,
    in_matrix,
    out_matrix,
    conv_taps,
    conv_bias,
    dt_bias,
    decay_log,
    skip_scale,
    mixer_gain,
    input_gain,
):
    units = inputs[0].astype(jnp.float32)
    seg_ids = segment_ids[0]
    length = units.shape[0]
    inv_rms = lax.rsqrt(jnp.mean(units * units, axis=-1, keepdims=True) + epsilon)
    base_rows = units * inv_rms
    w_piece = lax.all_gather(in_matrix, "fsdp", axis=0, tiled=True)
    g_piece = lax.all_gather(input_gain, "fsdp", axis=0, tiled=True)
    g_float = g_piece.astype(jnp.float32)
    part_rows = (base_rows * g_float).astype(jnp.bfloat16)
    product = jnp.dot(part_rows, w_piece, preferred_element_type=jnp.float32)
    projected = product
    projected = projected.astype(jnp.bfloat16)
    gate_part = projected[:, :INNER].astype(jnp.float32)
    conv_input = projected[:, INNER : INNER + XBC]
    dt_raw = projected[:, INNER + XBC :].astype(jnp.float32)
    out_whole, taps_whole, bias_whole, dtb_whole, decay_whole, skip_whole, norm_whole = (
        lax.all_gather(out_matrix, "fsdp", axis=0, tiled=True),
        lax.all_gather(conv_taps, "fsdp", axis=0, tiled=True),
        lax.all_gather(conv_bias, "fsdp", axis=0, tiled=True),
        lax.all_gather(dt_bias, "fsdp", axis=0, tiled=True),
        lax.all_gather(decay_log, "fsdp", axis=0, tiled=True),
        lax.all_gather(skip_scale, "fsdp", axis=0, tiled=True),
        lax.all_gather(mixer_gain, "fsdp", axis=0, tiled=True),
    )
    rim_rows, rim_seg = passed_along(
        (conv_input[length - CONV + 1 :], seg_ids[length - CONV + 1 :]), "ctx", 1
    )
    ext_rows = jnp.concatenate([rim_rows, conv_input], axis=0).astype(jnp.float32)
    seg_ext = jnp.concatenate([rim_seg, seg_ids], axis=0)
    seg_start = rim_seg[CONV - 2]

    def front_fn(ext_arg, dt_arg, taps_arg, bias_arg, dtb_arg, decay_arg):
        return mixer_front(
            ext_arg, dt_arg, taps_arg, bias_arg, dtb_arg, decay_arg, seg_ext, seg_ids, seg_start
        )

    front_out, front_back = jax.vjp(
        front_fn,
        ext_rows,
        dt_raw,
        taps_whole.astype(jnp.float32),
        bias_whole.astype(jnp.float32),
        dtb_whole.astype(jnp.float32),
        decay_whole.astype(jnp.float32),
    )
    values, c_rows, running, y_local, carried, retain = front_out
    identity = (jnp.ones((HEADS,), jnp.float32), jnp.zeros((HEADS, HDIM, STATE), jnp.float32))
    passed = prefix((retain, carried), "ctx", combine, identity)
    carried_in = passed[1]
    carry_flag = (seg_ids == seg_start).astype(jnp.float32)

    def tail_fn(
        values_arg, c_arg, running_arg, local_arg, carried_arg, gate_arg, skip_arg, gain_arg
    ):
        return mixer_tail(
            values_arg,
            c_arg,
            running_arg,
            local_arg,
            carried_arg,
            gate_arg,
            skip_arg,
            gain_arg,
            carry_flag,
        )

    mixer_out, tail_back = jax.vjp(
        tail_fn,
        values,
        c_rows,
        running,
        y_local,
        carried_in,
        gate_part,
        skip_whole.astype(jnp.float32),
        norm_whole.astype(jnp.float32),
    )
    mixer_low = mixer_out.astype(jnp.bfloat16)
    mixed = jnp.dot(mixer_low, out_whole, preferred_element_type=jnp.float32)
    summed_out = units + mixed
    block_out = summed_out.astype(jnp.bfloat16)
    cot_rows = out_grad[0]
    d_out_matrix = lax.dot_general(
        mixer_low, cot_rows, (((0,), (0,)), ((), ())), preferred_element_type=jnp.float32
    )
    d_mixer = lax.dot_general(
        cot_rows, out_whole, (((1,), (1,)), ((), ())), preferred_element_type=jnp.float32
    )
    d_values, d_c_rows, d_running, d_local, d_carried, d_gate, d_skip, d_norm_gain = tail_back(
        d_mixer
    )
    reversed_pair = prefix_2((retain, d_carried), "ctx", combine, identity)
    d_state = reversed_pair[1]
    d_retain = jnp.sum(d_state * carried_in, axis=(1, 2))
    d_ext, d_dt_raw, d_taps, d_bias, d_dtb, d_decay = front_back(
        (d_values, d_c_rows, d_running, d_local, d_state, d_retain)
    )
    returned = passed_along(d_ext[: CONV - 1].astype(jnp.bfloat16), "ctx", -1).astype(jnp.float32)
    d_conv_in = jnp.concatenate([d_ext[CONV - 1 : length], d_ext[length:] + returned], axis=0)
    d_projected = jnp.concatenate([d_gate, d_conv_in, d_dt_raw], axis=1).astype(jnp.bfloat16)
    d_in_matrix = lax.dot_general(
        part_rows, d_projected, (((0,), (0,)), ((), ())), preferred_element_type=jnp.float32
    )
    d_normed = lax.dot_general(
        d_projected,
        lax.all_gather(in_matrix, "fsdp", axis=0, tiled=True),
        (((1,), (1,)), ((), ())),
        preferred_element_type=jnp.float32,
    )
    d_input_gain = jnp.sum(d_normed * base_rows, axis=0)
    d_base = d_normed * g_float
    d_units = inv_rms * (d_base - base_rows * jnp.mean(d_base * base_rows, axis=-1, keepdims=True))
    input_grad = (cot_rows.astype(jnp.float32) + d_units).astype(jnp.bfloat16)
    split_sums = (
        lax.psum_scatter(
            d_in_matrix.astype(jnp.bfloat16), "fsdp", scatter_dimension=0, tiled=True
        ).astype(jnp.float32),
        lax.psum_scatter(
            d_out_matrix.astype(jnp.bfloat16), "fsdp", scatter_dimension=0, tiled=True
        ).astype(jnp.float32),
        lax.psum_scatter(
            d_taps.astype(jnp.bfloat16), "fsdp", scatter_dimension=0, tiled=True
        ).astype(jnp.float32),
        lax.psum_scatter(
            d_bias.astype(jnp.bfloat16), "fsdp", scatter_dimension=0, tiled=True
        ).astype(jnp.float32),
        lax.psum_scatter(
            d_norm_gain.astype(jnp.bfloat16), "fsdp", scatter_dimension=0, tiled=True
        ).astype(jnp.float32),
        lax.psum_scatter(
            d_input_gain.astype(jnp.bfloat16), "fsdp", scatter_dimension=0, tiled=True
        ).astype(jnp.float32),
    )
    reduced = (
        lax.psum(split_sums[0].astype(jnp.bfloat16), "ctx").astype(jnp.float32),
        lax.psum(split_sums[1].astype(jnp.bfloat16), "ctx").astype(jnp.float32),
        lax.psum(split_sums[2].astype(jnp.bfloat16), "ctx").astype(jnp.float32),
        lax.psum(split_sums[3].astype(jnp.bfloat16), "ctx").astype(jnp.float32),
        lax.psum(split_sums[4].astype(jnp.bfloat16), "ctx").astype(jnp.float32),
        lax.psum(split_sums[5].astype(jnp.bfloat16), "ctx").astype(jnp.float32),
    )
    square_sums = jnp.stack([jnp.sum(summed_out * summed_out), jnp.sum(mixed * mixed)])
    head_dt, head_decay, head_skip, stat_sums = lax.psum(
        (d_dtb, d_decay, d_skip, square_sums), ("fsdp", "ctx")
    )
    per_shard = HEADS // lax.axis_size("fsdp")
    offset_rows = lax.axis_index("fsdp") * per_shard
    dt_grad = lax.dynamic_slice_in_dim(head_dt, offset_rows, per_shard, 0)
    decay_grad = lax.dynamic_slice_in_dim(head_decay, offset_rows, per_shard, 0)
    skip_grad = lax.dynamic_slice_in_dim(head_skip, offset_rows, per_shard, 0)
    entries = length * lax.axis_size("fsdp") * lax.axis_size("ctx") * D
    rms_stats = jnp.sqrt(stat_sums / entries)
    return (
        block_out[None],
        input_grad[None],
        reduced[0],
        reduced[1],
        reduced[2],
        reduced[3],
        dt_grad,
        decay_grad,
        skip_grad,
        reduced[4],
        reduced[5],
        rms_stats,
    )


def solution(mesh):
    return jax.shard_map(
        on_device,
        mesh=mesh,
        in_specs=(
            P("fsdp", "ctx", None),
            P("fsdp", "ctx"),
            P("fsdp", "ctx", None),
            P("fsdp", None),
            P("fsdp", None),
            P("fsdp", None),
            P("fsdp"),
            P("fsdp"),
            P("fsdp"),
            P("fsdp"),
            P("fsdp"),
            P("fsdp"),
        ),
        out_specs=(
            P("fsdp", "ctx", None),
            P("fsdp", "ctx", None),
            P("fsdp", None),
            P("fsdp", None),
            P("fsdp", None),
            P("fsdp"),
            P("fsdp"),
            P("fsdp"),
            P("fsdp"),
            P("fsdp"),
            P("fsdp"),
            P(),
        ),
        check_vma=False,
    )
```

profile of v0, /device:TPU:0, one launch (start us, length us, event | category | flops | bytes accessed | tf_op | source)
XLA Modules:
  0.0 1636.9 jit_solution(982712403689798339)
XLA Ops:
  25.6 8.2 all-reduce.24
  33.8 5.5 all-gather.3
  44.6 93.2 %all-gather.11.cloned.1.call-done = bf16[1536,6448]{0,1:T(8,128)(2,1)} async-done(((bf16[384,6448]{0,1:T(8,128)(2,1)}), bf16[1536,6448]{0,1:T(8,128)(2,1)}) %all-gather.11.cloned.1.call-update) | async-done | bytes 19808272 | tf_op jit(solution)/shard_map/all_gather | solution.py:177
  137.8 16.7 %convolution_convert_fusion.2 = bf16[512,6448]{1,0:T(8,128)(2,1)} fusion(bf16[1536,6448]{0,1:T(8,128)(2,1)} %all-gather.11.cloned.1.call-done, bf16[1,512,1536]{2,1,0:T(8,128)(2,1)S(1)} %copy-done.14, f32[1536]{0:T(1024)S(1)} %reshape.551, f32[512]{0:T(512)S(1)} %add_rsqrt_fusion), kind=kOutput, calls=%fused_computation.150 | convolution fusion | flops 10148274176 | bytes 27992064 | tf_op jit(solution)/shard_map/dot_general | solution.py:181
  167.6 8.4 fusion.93
  175.9 6.1 slice.212
  183.9 6.6 copy.271
  190.5 8.2 reshape.509
  198.7 6.3 copy.274
  205.0 210.1 %while.80 = (s32[]{:T(128)}, f32[48,64,128]{2,1,0:T(8,128)S(1)}, s32[]{:T(128)}, f32[48]{0:T(128)S(1)}, f32[2,256,48,64]{1,0,3,2:T(2,128)}, /*index=5*/f32[2,256...) while((s32[]{:T(128)}, f32[48,64,128]{2,1,0:T(8,128)S(1)}, ...), condition=%wide.region_4.5_spmd.clone, body=%wide.region_1.4_spmd.clone.sunk | while | flops 4951254016 | bytes 38503760 | solution.py:119
  208.6 16.5 %fusion.240 = f32[48,64,256]{2,1,0:T(8,128)} fusion(f32[48,256]{1,0:T(8,128)S(1)} %dynamic-slice_bitcast_fusion.17, f32[256,256]{1,0:T(8,128)S(1)} %fusion.238, f32[48,256]{1,0:T(8,128)S(1)} %get-tuple-element.1556, pred[256,256]{1,0:T(8,128)(4,1)S(1)} %fusion.239, f32[2,256,48,64]{1,3,2,0:T(8,128)} %get-tuple-element.1663, s32[]{:T(128)} %get-tuple-element.1634), kind=kOutput, calls=%fused_computation.6.clone.1 | convolution fusion | flops 2428502016 | bytes 6767104 | tf_op jit(solution)/shard_map/jvp()/while/body/eval_jaxpr/hts,shp->thp/dot_general | solution.py:82
  236.9 63.6 %dynamic_update_slice.95 = f32[2,256,48,64]{1,0,3,2:T(2,128)} dynamic-update-slice(f32[2,256,48,64]{1,0,3,2:T(2,128)} %get-tuple-element.1638, f32[1,256,48,64]{1,0,3,2:T(1,128)} %copy.397, s32[]{:T(128)} %get-tuple-element.1634, s32[]{:T(128)} %constant.198.clone.1..sunk.1, s32[]{:T(128)} %constant.198.clone.1..sunk.1, s32[]{:T(128)} %constant.198.clone.1..sunk.1) | dynamic-update-slice | bytes 6291460 | tf_op jit(solution)/shard_map/jvp()/while/body/jit(dynamic_update_index_in_dim)/dynamic_update_slice | solution.py:119
  313.4 16.5 %fusion.240 = f32[48,64,256]{2,1,0:T(8,128)} fusion(f32[48,256]{1,0:T(8,128)S(1)} %dynamic-slice_bitcast_fusion.17, f32[256,256]{1,0:T(8,128)S(1)} %fusion.238, f32[48,256]{1,0:T(8,128)S(1)} %get-tuple-element.1556, pred[256,256]{1,0:T(8,128)(4,1)S(1)} %fusion.239, f32[2,256,48,64]{1,3,2,0:T(8,128)} %get-tuple-element.1663, s32[]{:T(128)} %get-tuple-element.1634), kind=kOutput, calls=%fused_computation.6.clone.1 | convolution fusion | flops 2428502016 | bytes 6767104 | tf_op jit(solution)/shard_map/jvp()/while/body/eval_jaxpr/hts,shp->thp/dot_general | solution.py:82
  341.7 63.6 %dynamic_update_slice.95 = f32[2,256,48,64]{1,0,3,2:T(2,128)} dynamic-update-slice(f32[2,256,48,64]{1,0,3,2:T(2,128)} %get-tuple-element.1638, f32[1,256,48,64]{1,0,3,2:T(1,128)} %copy.397, s32[]{:T(128)} %get-tuple-element.1634, s32[]{:T(128)} %constant.198.clone.1..sunk.1, s32[]{:T(128)} %constant.198.clone.1..sunk.1, s32[]{:T(128)} %constant.198.clone.1..sunk.1) | dynamic-update-slice | bytes 6291460 | tf_op jit(solution)/shard_map/jvp()/while/body/jit(dynamic_update_index_in_dim)/dynamic_update_slice | solution.py:119
  417.6 5.2 all-gather.5
  425.2 18.4 %all-gather.4 = bf16[8,1,48]{2,1,0:T(2,128)(2,1)S(1)} all-gather(bf16[1,1,48]{2,1,0:T(2,128)(2,1)S(1)} %bitcast.512), channel_id=1, replica_groups=mesh['fsdp'=4,'ctx'=8] {'ctx'}, dimensions={0}, use_global_device_ids=true | all-gather | bytes 864 | tf_op jit(solution)/shard_map/all_gather | solution.py:27
  443.6 9.0 reshape.512
  452.6 61.9 %all-gather.15.cloned.1.call-done = bf16[384,64,128]{2,1,0:T(8,128)(2,1)} async-done(((bf16[48,64,128]{2,1,0:T(8,128)(2,1)}), bf16[384,64,128]{2,1,0:T(8,128)(2,1)}) %all-gather.15.cloned.1.call-update) | async-done | bytes 6291472 | tf_op jit(solution)/shard_map/all_gather | solution.py:27
  514.7 13.1 multiply_add_fusion.4
  527.8 6.6 copy.278
  534.4 6.8 multiply_reduce_fusion.13
  541.2 37.4 %all-gather.13.cloned.1.call-done = bf16[3072,1536]{1,0:T(8,128)(2,1)} async-done(((bf16[768,1536]{1,0:T(8,128)(2,1)}), bf16[3072,1536]{1,0:T(8,128)(2,1)}) %all-gather.13.cloned.1.call-update) | async-done | bytes 9437200 | tf_op jit(solution)/shard_map/all_gather | solution.py:188
  578.6 12.5 multiply_reduce_fusion.9
  591.1 11.2 multiply_reduce_fusion.10
  602.3 6.5 copy.280
  608.8 8.2 fusion.126
  617.9 10.2 reshape.581
  628.0 11.0 copy.286
  639.0 6.4 multiply_reduce_fusion.11
  645.4 70.8 %all-gather.17.cloned.1.call-done = bf16[384,64,128]{2,1,0:T(8,128)(2,1)} async-done(((bf16[48,64,128]{2,1,0:T(8,128)(2,1)}), bf16[384,64,128]{2,1,0:T(8,128)(2,1)}) %all-gather.17.cloned.1.call-update) | async-done | bytes 6291472 | tf_op jit(solution)/shard_map/all_gather | solution.py:47
  716.2 24.0 %while.81 = (s32[]{:T(128)}, f32[48,64,128]{2,1,0:T(8,128)}, s32[]{:T(128)}, bf16[8,48]{1,0:T(8,128)(2,1)S(1)}, bf16[8,48,64,128]{3,2,1,0:T(8,128)(2,1)}, /*index=5*/s32[]{:T(128)}, s32[]{:T(128)}, s32[]{:T(128)}, s32[]{:T(128)}) while((s32[]{:T(128)}, f32[48,64,128]{2,1,0:T(8,128)}, s32[]{:T(128)}, ...), condition=%wide.region_10.11_spmd.clone, body=%wide.region_9.10_spmd.clone.sunk | while | flops 1966136 | bytes 3932807 | solution.py:63
  749.2 248.0 %while.82 = (s32[]{:T(128)}, f32[48,64,128]{2,1,0:T(8,128)}, f32[48]{0:T(128)}, f32[2,256,48,64]{1,3,2,0:T(8,128)}, f32[2,256,128]{2,1,0:T(8,128)}, /*index=5*/f...) while((s32[]{:T(128)}, f32[48,64,128]{2,1,0:T(8,128)}, ...), condition=%wide.region_26.27_spmd.clone, body=%wide.region_13.26_spmd.clone.sunk | while | flops 11239392256 | bytes 115198616 | solution.py:119
  769.1 5.3 dynamic-slice_bitcast_fusion.19
  785.5 6.7 multiply_reduce_fusion.21
  809.2 21.4 %fusion.264 = (f32[48,256]{1,0:T(8,128)S(1)}, f32[48,256]{1,0:T(8,128)S(1)}, f32[48,256]{1,0:T(8,128)}, f32[256,256]{1,0:T(8,128)}) fusion(f32[48,256]{1,0:T(8,128)S(1)} %bitcast.484, f32[256,256]{1,0:T(8,128)S(1)} %fusion.262, f32[48,256]{1,0:T(8,128)} %get-tuple-element.1594, pred[256,256]{1,0:T(8,128)(4,1)S(1)} %fusion.263, ...), kind=kOutput, calls=%fused_computation.72.clone.1 | convolution fusion | flops 2456711168 | bytes 7127040 | tf_op jit(solution)/shard_map/transpose(jvp())/while/body/eval_jaxpr/checkpoint/hts,shp->thp/dot_general | solution.py:82
  844.3 6.4 fusion.269
  852.8 6.5 fusion.267
  860.7 12.2 bitcast_dynamic-update-slice_fusion.7
  878.7 5.3 dynamic-slice_bitcast_fusion.19
  895.7 6.7 multiply_reduce_fusion.21
  919.4 21.4 %fusion.264 = (f32[48,256]{1,0:T(8,128)S(1)}, f32[48,256]{1,0:T(8,128)S(1)}, f32[48,256]{1,0:T(8,128)}, f32[256,256]{1,0:T(8,128)}) fusion(f32[48,256]{1,0:T(8,128)S(1)} %bitcast.484, f32[256,256]{1,0:T(8,128)S(1)} %fusion.262, f32[48,256]{1,0:T(8,128)} %get-tuple-element.1594, pred[256,256]{1,0:T(8,128)(4,1)S(1)} %fusion.263, ...), kind=kOutput, calls=%fused_computation.72.clone.1 | convolution fusion | flops 2456711168 | bytes 7127040 | tf_op jit(solution)/shard_map/transpose(jvp())/while/body/eval_jaxpr/checkpoint/hts,shp->thp/dot_general | solution.py:82
  954.6 6.4 fusion.269
  963.0 6.5 fusion.267
  971.0 12.2 bitcast_dynamic-update-slice_fusion.7
  997.2 12.7 fusion.132
  1009.9 11.3 copy.299
  1021.2 10.8 reshape.582
  1032.0 6.0 multiply_add_fusion.3
  1038.1 10.7 multiply_reduce_fusion.8
  1048.8 8.2 broadcast_multiply_fusion
  1057.0 8.0 fusion.165
  1075.3 16.4 convolution_convert_fusion
  1091.6 24.2 %copy.300 = bf16[1536,6448]{1,0:T(8,128)(2,1)} copy(bf16[1536,6448]{0,1:T(8,128)(2,1)} %convolution_convert_fusion) | data formatting | bytes 39616512
  1117.2 11.2 convolution_convert_fusion.1
  1130.3 133.6 %reduce-scatter.10.cloned.1.call-done = bf16[384,6448]{1,0:T(8,128)(2,1)} async-done(((bf16[1536,6448]{1,0:T(8,128)(2,1)}), bf16[384,6448]{1,0:T(8,128)(2,1)}) %reduce-scatter.10.cloned.1.call-update) | async-done | bytes 4952080
  1264.0 7.6 copy.301
  1271.5 74.1 %reduce-scatter.8.cloned.1.call-done = bf16[768,1536]{1,0:T(8,128)(2,1)} async-done(((bf16[3072,1536]{1,0:T(8,128)(2,1)}), bf16[768,1536]{1,0:T(8,128)(2,1)}) %reduce-scatter.8.cloned.1.call-update) | async-done | bytes 2359312 | tf_op jit(solution)/shard_map/reduce_scatter | solution.py:289
  1348.0 20.0 %fusion.135 = f32[512,1536]{1,0:T(8,128)S(1)} fusion(bf16[1536,6448]{0,1:T(8,128)(2,1)} %all-gather.11.cloned.1.call-done, bf16[512,48]{1,0:T(8,128)(2,1)S(1)} %copy-done.49, bf16[3,3328]{1,0:T(4,128)(2,1)S(1)} %fusion.147, bf16[509,3328]{1,0:T(8,128)(2,1)} %copy-done.19, bf16[512,3072]{1,0:T(8,128)(2,1)} %get-tuple-element.1248), kind=kOutput, calls=%fused_computation.222 | convolution fusion | flops 10168238080 | bytes 29556736 | tf_op jit(solution)/shard_map/dot_general | solution.py:275
  1368.1 12.7 multiply_reduce_fusion.15
  1382.2 44.0 %all-reduce.20 = (f32[48]{0:T(128)S(1)}, f32[48]{0:T(128)S(1)}, f32[48]{0:T(128)S(1)}, f32[2]{0:T(128)S(1)}) all-reduce(f32[48]{0:T(128)S(1)} %copy-done.80, f32[48]{0:T(128)S(1)} %fusion.156, f32[48]{0:T(128)S(1)} %reduce_sum.376, f32[2]{0:T(128)S(1)} %pad_maximum_fusion.3), channel_id=1, replica_groups=mesh['fsdp'=4,'ctx'=8] {'fsdp','ctx'}, use_global_device_ids=true, to_apply=%region_42.43 | all-reduce | flops 146 | bytes 1168 | tf_op jit(solution)/shard_map/psum | solution.py:314
  1427.9 11.9 all-reduce.23
  1446.5 37.0 %all-reduce.21 = (bf16[832,4]{0,1:T(4,128)(2,1)S(1)}, bf16[832]{0:T(1024)(128)(2,1)S(1)}, bf16[768]{0:T(1024)(128)(2,1)S(1)}, bf16[384]{0:T(512)(128)(2,1)S(1)}) all-reduce(bf16[832,4]{0,1:T(4,128)(2,1)S(1)} %copy.303, bf16[832]{0:T(1024)(128)(2,1)S(1)} %dynamic-slice.5, ...), channel_id=1, replica_groups=mesh['fsdp'=4,'ctx'=8] {'ctx'}, use_global_device_ids=true, to_apply=%region_37.38 | all-reduce | flops 5312 | bytes 21248 | tf_op jit(solution)/shard_map/psum | solution.py:308
  1485.9 133.8 %all-reduce.27.cloned.1.call-done = (bf16[384,6448]{0,1:T(8,128)(2,1)}, bf16[768,1536]{1,0:T(8,128)(2,1)}) async-done(((bf16[384,6448]{0,1:T(8,128)(2,1)}, bf16[768,1536]{1,0:T(8,128)(2,1)}), (bf16[384,6448]{0,1:T(8,128)(2,1)}, bf16[768,1536]{1,0:T(8,128)(2,1)})) %all-reduce.27.cloned.1.call-update) | async-done | bytes 7311376 | tf_op jit(solution)/shard_map/psum | solution.py:306
  1619.7 7.1 convert_element_type.263
  (495 shorter events, 248.6 us)
Async XLA Ops:
  7.2 36.1 %copy-start.68 = (s32[1,512]{1,0:T(1,128)S(1)}, s32[1,512]{1,0:T(1,128)}, u32[]{:S(2)}) copy-start(s32[1,512]{1,0:T(1,128)} %param.21) | copy-start | bytes 6148
  7.2 34.3 %copy-start.14 = (bf16[1,512,1536]{2,1,0:T(8,128)(2,1)S(1)}, bf16[1,512,1536]{2,1,0:T(8,128)(2,1)}, u32[]{:S(2)}) copy-start(bf16[1,512,1536]{2,1,0:T(8,128)(2,1)} %param.20) | copy-start | bytes 4718596
  7.2 130.6 %all-gather.11.cloned.1.call-start = ((), (), s32[]{:S(2)}) async-start(), calls=%async_computation.3 | async-start | bytes 24760320 | tf_op jit(solution)/shard_map/all_gather | solution.py:177
  7.9 506.6 %all-gather.15.cloned.1.call-start = ((), (), s32[]{:S(2)}) async-start(), calls=%async_computation.6 | async-start | bytes 7077888 | tf_op jit(solution)/shard_map/all_gather | solution.py:27
  8.7 33.3 %collective-permute-start = (s32[3]{0:T(128)S(1)}, s32[3]{0:T(128)S(1)}, u32[]{:S(2)}, u32[]{:S(2)}) collective-permute-start(s32[3]{0:T(128)S(1)} %slice_bitcast_fusion), channel_id=1, source_target_pairs={{0,1},{1,2},{2,3},{3,4},{4,5},{5,6},{6,7},{8,9},{9,10},{10,11},{11... | collective-permute-start | bytes 44 | tf_op jit(solution)/shard_map/ppermute | solution.py:21
  19.5 135.0 %copy-start.65 = (f32[1536]{0:T(1024)}, f32[1536]{0:T(1024)S(1)}, u32[]{:S(2)}) copy-start(f32[1536]{0:T(1024)S(1)} %reshape.551) | copy-start | bytes 18436
  33.8 120.7 %copy-start.83 = (bf16[48]{0:T(256)(128)(2,1)}, bf16[48]{0:T(256)(128)(2,1)S(1)}, u32[]{:S(2)}) copy-start(bf16[48]{0:T(256)(128)(2,1)S(1)} %get-tuple-element.1206) | copy-start | bytes 292
  39.5 119.4 %copy-start.76 = (f32[48]{0:T(128)}, f32[48]{0:T(128)S(1)}, u32[]{:S(2)}) copy-start(f32[48]{0:T(128)S(1)} %convert_element_type.241) | copy-start | bytes 580
  41.5 126.0 %copy-start.40 = (f32[3328]{0:T(1024)}, f32[3328]{0:T(1024)S(1)}, u32[]{:S(2)}) copy-start(f32[3328]{0:T(1024)S(1)} %get-tuple-element.1104) | copy-start | bytes 39940
  41.5 126.0 %copy-start.42 = (f32[3328]{0:T(1024)}, f32[3328]{0:T(1024)S(1)}, u32[]{:S(2)}) copy-start(f32[3328]{0:T(1024)S(1)} %get-tuple-element.1105) | copy-start | bytes 39940
  41.6 126.0 %copy-start.44 = (f32[3328]{0:T(1024)}, f32[3328]{0:T(1024)S(1)}, u32[]{:S(2)}) copy-start(f32[3328]{0:T(1024)S(1)} %get-tuple-element.1106) | copy-start | bytes 39940
  41.6 126.0 %copy-start.46 = (f32[3328]{0:T(1024)}, f32[3328]{0:T(1024)S(1)}, u32[]{:S(2)}) copy-start(f32[3328]{0:T(1024)S(1)} %get-tuple-element.1107) | copy-start | bytes 39940
  42.0 117.0 %copy-start.78 = (f32[48]{0:T(128)}, f32[48]{0:T(128)S(1)}, u32[]{:S(2)}) copy-start(f32[48]{0:T(128)S(1)} %convert_exponential_fusion) | copy-start | bytes 580
  42.0 112.5 %copy-start.73 = (f32[512]{0:T(512)}, f32[512]{0:T(512)S(1)}, u32[]{:S(2)}) copy-start(f32[512]{0:T(512)S(1)} %add_rsqrt_fusion) | copy-start | bytes 6148
  44.6 123.0 %copy-start.59 = (f32[512]{0:T(512)}, f32[512]{0:T(512)S(1)}, u32[]{:S(2)}) copy-start(f32[512]{0:T(512)S(1)} %get-tuple-element.1259) | copy-start | bytes 6148
  44.6 123.0 %copy-start.61 = (f32[512]{0:T(512)}, f32[512]{0:T(512)S(1)}, u32[]{:S(2)}) copy-start(f32[512]{0:T(512)S(1)} %get-tuple-element.1260) | copy-start | bytes 6148
  44.6 123.0 %copy-start.63 = (f32[512]{0:T(512)}, f32[512]{0:T(512)S(1)}, u32[]{:S(2)}) copy-start(f32[512]{0:T(512)S(1)} %get-tuple-element.1261) | copy-start | bytes 6148
  155.3 9.5 collective-permute-start.1
  205.0 212.5 %copy-start.81 = (bf16[768]{0:T(1024)(128)(2,1)S(1)}, bf16[768]{0:T(1024)(128)(2,1)}, u32[]{:S(2)}) copy-start(bf16[768]{0:T(1024)(128)(2,1)} %param.30) | copy-start | bytes 4612
  415.1 37.5 %copy-start.50 = (s32[2,256]{1,0:T(2,128)}, s32[2,256]{1,0:T(2,128)S(1)}, u32[]{:S(2)}) copy-start(s32[2,256]{1,0:T(2,128)S(1)} %get-tuple-element.1822) | copy-start | bytes 6148
  416.2 162.4 %all-gather.13.cloned.1.call-start = ((), (), s32[]{:S(2)}) async-start(), calls=%async_computation.4 | async-start | bytes 11796480 | tf_op jit(solution)/shard_map/all_gather | solution.py:188
  416.9 299.3 %all-gather.17.cloned.1.call-start = ((), (), s32[]{:S(2)}) async-start(), calls=%async_computation.7 | async-start | bytes 7077888 | tf_op jit(solution)/shard_map/all_gather | solution.py:47
  422.7 168.4 %copy-start.55 = (f32[4,1,768]{2,1,0:T(1,128)}, f32[4,1,768]{2,1,0:T(1,128)S(1)}, u32[]{:S(2)}) copy-start(f32[4,1,768]{2,1,0:T(1,128)S(1)} %convert_element_type.281) | copy-start | bytes 36868
  452.6 156.2 %copy-start.24 = (f32[512,48]{0,1:T(8,128)}, f32[512,48]{0,1:T(8,128)S(1)}, u32[]{:S(2)}) copy-start(f32[512,48]{0,1:T(8,128)S(1)} %exponential_multiply_fusion.4) | copy-start | bytes 294916
  514.7 225.5 %copy-start.2 = (f32[48,64,128]{2,1,0:T(8,128)}, f32[48,64,128]{2,1,0:T(8,128)S(1)}, u32[]{:S(2)}) copy-start(f32[48,64,128]{2,1,0:T(8,128)S(1)} %get-tuple-element.688) | copy-start | bytes 4718596
  534.4 44.2 %copy-start.27 = (bf16[1,512,1536]{2,1,0:T(8,128)(2,1)S(1)}, bf16[1,512,1536]{2,1,0:T(8,128)(2,1)}, u32[]{:S(2)}) copy-start(bf16[1,512,1536]{2,1,0:T(8,128)(2,1)} %param.22) | copy-start | bytes 4718596
  541.2 49.9 %copy-start.71 = (f32[512]{0:T(512)}, f32[512]{0:T(512)S(1)}, u32[]{:S(2)}) copy-start(f32[512]{0:T(512)S(1)} %fusion.153) | copy-start | bytes 6148
  617.1 646.9 %reduce-scatter.10.cloned.1.call-start = ((), (), s32[]{:S(2)}) async-start(), calls=%async_computation.8 | async-start | bytes 25067520
  776.8 32.3 %copy-start.8 = (f32[256,48]{0,1:T(8,128)}, f32[256,48]{0,1:T(8,128)S(1)}, u32[]{:S(2)}) copy-start(f32[256,48]{0,1:T(8,128)S(1)} %get-tuple-element.1590) | copy-start | bytes 147460 | tf_op jit(solution)/shard_map/transpose(jvp())/while
  808.3 22.4 %copy-start.12 = (f32[256,256]{1,0:T(8,128)}, f32[256,256]{1,0:T(8,128)S(1)}, u32[]{:S(2)}) copy-start(f32[256,256]{1,0:T(8,128)S(1)} %fusion.262) | copy-start | bytes 786436 | tf_op jit(solution)/shard_map/transpose(jvp())/while
  809.1 21.5 %copy-start.25 = (pred[256,256]{1,0:T(8,128)(4,1)}, pred[256,256]{1,0:T(8,128)(4,1)S(1)}, u32[]{:S(2)}) copy-start(pred[256,256]{1,0:T(8,128)(4,1)S(1)} %fusion.263) | copy-start | bytes 196612 | tf_op jit(solution)/shard_map/transpose(jvp())/while
  809.1 21.5 %copy-start.18 = (f32[1,256,48]{1,2,0:T(8,128)S(1)}, f32[1,256,48]{1,2,0:T(8,128)}, u32[]{:S(2)}) copy-start(f32[1,256,48]{1,2,0:T(8,128)} %copy.405) | copy-start | bytes 147460 | tf_op jit(solution)/shard_map/transpose(jvp())/while
  809.2 21.5 %copy-start.22 = (f32[1,48]{0,1:T(8,128)S(1)}, f32[1,48]{0,1:T(8,128)}, u32[]{:S(2)}) copy-start(f32[1,48]{0,1:T(8,128)} %copy.406) | copy-start | bytes 580 | tf_op jit(solution)/shard_map/transpose(jvp())/while
  809.2 21.5 %copy-start.35 = (f32[48,2]{0,1:T(2,128)S(1)}, f32[48,2]{0,1:T(2,128)}, u32[]{:S(2)}) copy-start(f32[48,2]{0,1:T(2,128)} %copy-done.34) | copy-start | bytes 1156 | tf_op jit(solution)/shard_map/transpose(jvp())/while
  809.2 21.5 %copy-start.36 = (f32[256]{0:T(256)S(1)}, f32[256]{0:T(256)}, u32[]{:S(2)}) copy-start(f32[256]{0:T(256)} %get-tuple-element.1602) | copy-start | bytes 3076 | tf_op jit(solution)/shard_map/transpose(jvp())/while
  809.2 21.5 %copy-start.39 = (f32[48]{0:T(128)S(1)}, f32[48]{0:T(128)}, u32[]{:S(2)}) copy-start(f32[48]{0:T(128)} %copy-done.38) | copy-start | bytes 580 | tf_op jit(solution)/shard_map/transpose(jvp())/while
  809.2 21.5 %copy-start.52 = (f32[256]{0:T(256)S(1)}, f32[256]{0:T(256)}, u32[]{:S(2)}) copy-start(f32[256]{0:T(256)} %get-tuple-element.1607) | copy-start | bytes 3076 | tf_op jit(solution)/shard_map/transpose(jvp())/while
  840.0 20.6 %copy-start.3 = (f32[256,48,64]{0,2,1:T(8,128)S(1)}, f32[256,48,64]{0,2,1:T(8,128)}, u32[]{:S(2)}) copy-start(f32[256,48,64]{0,2,1:T(8,128)} %get-tuple-element.1611) | copy-start | bytes 9437188 | tf_op jit(solution)/shard_map/transpose(jvp())/while
  840.0 20.6 %copy-start.9 = (f32[256,48]{0,1:T(8,128)S(1)}, f32[256,48]{0,1:T(8,128)}, u32[]{:S(2)}) copy-start(f32[256,48]{0,1:T(8,128)} %copy-done.8) | copy-start | bytes 147460 | tf_op jit(solution)/shard_map/transpose(jvp())/while
  840.0 20.6 %copy-start.13 = (f32[256,256]{1,0:T(8,128)S(1)}, f32[256,256]{1,0:T(8,128)}, u32[]{:S(2)}) copy-start(f32[256,256]{1,0:T(8,128)} %copy-done.12) | copy-start | bytes 786436 | tf_op jit(solution)/shard_map/transpose(jvp())/while
  886.4 33.0 %copy-start.8 = (f32[256,48]{0,1:T(8,128)}, f32[256,48]{0,1:T(8,128)S(1)}, u32[]{:S(2)}) copy-start(f32[256,48]{0,1:T(8,128)S(1)} %get-tuple-element.1590) | copy-start | bytes 147460 | tf_op jit(solution)/shard_map/transpose(jvp())/while
  918.5 22.4 %copy-start.12 = (f32[256,256]{1,0:T(8,128)}, f32[256,256]{1,0:T(8,128)S(1)}, u32[]{:S(2)}) copy-start(f32[256,256]{1,0:T(8,128)S(1)} %fusion.262) | copy-start | bytes 786436 | tf_op jit(solution)/shard_map/transpose(jvp())/while
  919.4 21.5 %copy-start.25 = (pred[256,256]{1,0:T(8,128)(4,1)}, pred[256,256]{1,0:T(8,128)(4,1)S(1)}, u32[]{:S(2)}) copy-start(pred[256,256]{1,0:T(8,128)(4,1)S(1)} %fusion.263) | copy-start | bytes 196612 | tf_op jit(solution)/shard_map/transpose(jvp())/while
  919.4 21.5 %copy-start.18 = (f32[1,256,48]{1,2,0:T(8,128)S(1)}, f32[1,256,48]{1,2,0:T(8,128)}, u32[]{:S(2)}) copy-start(f32[1,256,48]{1,2,0:T(8,128)} %copy.405) | copy-start | bytes 147460 | tf_op jit(solution)/shard_map/transpose(jvp())/while
  919.4 21.5 %copy-start.22 = (f32[1,48]{0,1:T(8,128)S(1)}, f32[1,48]{0,1:T(8,128)}, u32[]{:S(2)}) copy-start(f32[1,48]{0,1:T(8,128)} %copy.406) | copy-start | bytes 580 | tf_op jit(solution)/shard_map/transpose(jvp())/while
  919.4 21.5 %copy-start.35 = (f32[48,2]{0,1:T(2,128)S(1)}, f32[48,2]{0,1:T(2,128)}, u32[]{:S(2)}) copy-start(f32[48,2]{0,1:T(2,128)} %copy-done.34) | copy-start | bytes 1156 | tf_op jit(solution)/shard_map/transpose(jvp())/while
  919.4 21.5 %copy-start.36 = (f32[256]{0:T(256)S(1)}, f32[256]{0:T(256)}, u32[]{:S(2)}) copy-start(f32[256]{0:T(256)} %get-tuple-element.1602) | copy-start | bytes 3076 | tf_op jit(solution)/shard_map/transpose(jvp())/while
  919.4 21.5 %copy-start.39 = (f32[48]{0:T(128)S(1)}, f32[48]{0:T(128)}, u32[]{:S(2)}) copy-start(f32[48]{0:T(128)} %copy-done.38) | copy-start | bytes 580 | tf_op jit(solution)/shard_map/transpose(jvp())/while
  919.4 21.5 %copy-start.52 = (f32[256]{0:T(256)S(1)}, f32[256]{0:T(256)}, u32[]{:S(2)}) copy-start(f32[256]{0:T(256)} %get-tuple-element.1607) | copy-start | bytes 3076 | tf_op jit(solution)/shard_map/transpose(jvp())/while
  950.3 20.7 %copy-start.3 = (f32[256,48,64]{0,2,1:T(8,128)S(1)}, f32[256,48,64]{0,2,1:T(8,128)}, u32[]{:S(2)}) copy-start(f32[256,48,64]{0,2,1:T(8,128)} %get-tuple-element.1611) | copy-start | bytes 9437188 | tf_op jit(solution)/shard_map/transpose(jvp())/while
  950.3 20.7 %copy-start.9 = (f32[256,48]{0,1:T(8,128)S(1)}, f32[256,48]{0,1:T(8,128)}, u32[]{:S(2)}) copy-start(f32[256,48]{0,1:T(8,128)} %copy-done.8) | copy-start | bytes 147460 | tf_op jit(solution)/shard_map/transpose(jvp())/while
  950.3 20.6 %copy-start.13 = (f32[256,256]{1,0:T(8,128)S(1)}, f32[256,256]{1,0:T(8,128)}, u32[]{:S(2)}) copy-start(f32[256,256]{1,0:T(8,128)} %copy-done.12) | copy-start | bytes 786436 | tf_op jit(solution)/shard_map/transpose(jvp())/while
  950.3 20.6 %copy-start.17 = (f32[256,48]{0,1:T(8,128)S(1)}, f32[256,48]{0,1:T(8,128)}, u32[]{:S(2)}) copy-start(f32[256,48]{0,1:T(8,128)} %get-tuple-element.1612) | copy-start | bytes 147460 | tf_op jit(solution)/shard_map/transpose(jvp())/while
  950.3 20.6 %copy-start.26 = (pred[256,256]{1,0:T(8,128)(4,1)S(1)}, pred[256,256]{1,0:T(8,128)(4,1)}, u32[]{:S(2)}) copy-start(pred[256,256]{1,0:T(8,128)(4,1)} %copy-done.25) | copy-start | bytes 196612 | tf_op jit(solution)/shard_map/transpose(jvp())/while
  1065.7 7.9 collective-permute-start.2
  1115.9 229.8 %reduce-scatter.8.cloned.1.call-start = ((), (), s32[]{:S(2)}) async-start(), calls=%async_computation.5 | async-start | bytes 11796480 | tf_op jit(solution)/shard_map/reduce_scatter | solution.py:289
  1128.5 317.0 %reduce-scatter.12.cloned.1.call-start = ((), (), s32[]{:S(2)}) async-start(), calls=%async_computation.9 | async-start | bytes 1064960
  1130.0 217.8 %copy-start.57 = (f32[3072]{0:T(1024)S(1)}, f32[3072]{0:T(1024)}, u32[]{:S(2)}) copy-start(f32[3072]{0:T(1024)} %get-tuple-element.1211) | copy-start | bytes 36868
  1130.0 218.0 %copy-start.82 = (f32[48]{0:T(128)S(1)}, f32[48]{0:T(128)}, u32[]{:S(2)}) copy-start(f32[48]{0:T(128)} %get-tuple-element.1249) | copy-start | bytes 580
  1130.0 218.0 %copy-start.84 = (bf16[48]{0:T(256)(128)(2,1)S(1)}, bf16[48]{0:T(256)(128)(2,1)}, u32[]{:S(2)}) copy-start(bf16[48]{0:T(256)(128)(2,1)} %copy-done.83) | copy-start | bytes 292
  1130.0 218.0 %copy-start.49 = (bf16[512,48]{1,0:T(8,128)(2,1)S(1)}, bf16[512,48]{1,0:T(8,128)(2,1)}, u32[]{:S(2)}) copy-start(bf16[512,48]{1,0:T(8,128)(2,1)} %copy-done.48) | copy-start | bytes 147460
  1130.0 489.6 %all-reduce.27.cloned.1.call-start = ((), (), s32[]{:S(2)}) async-start(), calls=%async_computation.10 | async-start | bytes 14622720 | tf_op jit(solution)/shard_map/psum | solution.py:306
  1345.7 22.4 %slice-start.2 = ((s8[6291456]{0:T(1024)(128)(4,1)}), s8[2097152]{0:T(1024)(128)(4,1)S(1)}, s32[]{:S(2)}) async-start(s8[6291456]{0:T(1024)(128)(4,1)} %bitcast.481), calls=%async_computation.13 | async-start | bytes 4194304
  1368.1 59.8 %copy-start.75 = (bf16[3072]{0:T(1024)(128)(2,1)S(1)}, bf16[3072]{0:T(1024)(128)(2,1)}, u32[]{:S(2)}) copy-start(bf16[3072]{0:T(1024)(128)(2,1)} %get-tuple-element.1095) | copy-start | bytes 18436
  (66 other events, 663.9 us)
Sparse Core Ops, SparseCore 0:
  9.6 128.1 all-gather.10
  416.3 98.1 all-gather.14
  516.1 62.4 all-gather.12
  617.2 99.0 all-gather.16
  1116.0 147.9 reduce-scatter.9
  1267.2 78.4 reduce-scatter.7
  1348.4 23.6 reduce-scatter.11
  1376.1 243.4 all-reduce.26
where the time goes:
time: 1660 us; the launch traced here: 1640 us
  waiting for transfers between devices  606 us (37%)
  local copies, waits for them, and re-layouts  345 us (21%)
  matrix products  310 us (19%)
  other arithmetic  174 us (10%)
  blocking collectives  135 us (8%)
  loops' own time  34.9 us (2%)
  between operations  20.9 us (1%)
    dynamic_update_slice x10, local copies, waits for them, and re-layouts, scan_ssd(): lax.scan(jax.checkpoint(block_step), initial, sliced)  142 us
    unnamed x10, waiting for transfers between devices  135 us
    psum x1, waiting for transfers between devices, on_device(): lax.psum(split_sums[0].astype(jnp.bfloat16), 'ctx').astype(jnp.float32)  134 us
    dot_general x6, matrix products, block_step(): y_diag = jnp.einsum('hts,shp->thp', mixing, xblock, precision=precise)  100 us
    all_gather x1, waiting for transfers between devices, on_device(): w_piece = lax.all_gather(in_matrix, 'fsdp', axis=0, tiled=True)  93.2 us
    reduce_scatter x1, waiting for transfers between devices, on_device(): lax.psum_scatter(d_out_matrix.astype(jnp.bfloat16), 'fsdp', scatter_dimen...  74.1 us
    all_gather x1, waiting for transfers between devices, prefix_2(): lax.all_gather(part.astype(kind), axis)  70.8 us
    all_gather x1, waiting for transfers between devices, prefix(): lax.all_gather(a.astype(kind), axis)  61.9 us
  transfers between devices with their start and end apart: 11, of which 7 were waited for; matrix products, arithmetic and copies ran while one was open for 9% of the time, Pallas kernels for 0%

commit v1 on v0

--- a/solution.py
+++ b/solution.py
@@ -174,7 +174,16 @@
     length = units.shape[0]
     inv_rms = lax.rsqrt(jnp.mean(units * units, axis=-1, keepdims=True) + epsilon)
     base_rows = units * inv_rms
-    w_piece = lax.all_gather(in_matrix, "fsdp", axis=0, tiled=True)
+    ways = lax.axis_size("fsdp")
+    up = [(d, (d + 1) % ways) for d in range(ways)]
+    down = [(d, (d - 1) % ways) for d in range(ways)]
+    earlier_2, later = ([in_matrix], [in_matrix])
+    for _ in range(ways // 2):
+        earlier_2.append(lax.ppermute(earlier_2[-1], "fsdp", up))
+    for _ in range((ways - 1) // 2):
+        later.append(lax.ppermute(later[-1], "fsdp", down))
+    line = jnp.concatenate([*earlier_2[::-1], *later[1:]], axis=0)
+    w_piece = jnp.roll(line, (lax.axis_index("fsdp") - ways // 2) * in_matrix.shape[0], axis=0)
     g_piece = lax.all_gather(input_gain, "fsdp", axis=0, tiled=True)
     g_float = g_piece.astype(jnp.float32)
     part_rows = (base_rows * g_float).astype(jnp.bfloat16)

time: 1660 us -> 1890 us (1.14)
  blocking collectives: 135 us -> 233 us
  waiting for transfers between devices: 606 us -> 696 us
  local copies, waits for them, and re-layouts: 345 us -> 383 us
    all_gather x1, blocking collectives: 5.14 us -> 103 us  [on_device(): g_piece = lax.all_gather(input_gain, 'fsdp', axis=0, tiled=True)]
    ppermute x0 -> x3, waiting for transfers between devices: none -> 56.6 us  [the longest x2 56.6 us: on_device(): earlier_2.append(lax.ppermute(earlier_2[-1], 'fsdp', up))]
    unnamed x143 -> x150, local copies, waits for them, and re-layouts: 61.7 us -> 94.1 us
    all_gather x1, waiting for transfers between devices: 93.2 us -> 124 us  [on_device(): lax.all_gather(in_matrix, 'fsdp', axis=0, tiled=True)]
  transfers between devices with their start and end apart: 11 -> 14, of which waited for: 7 -> 8; matrix products, arithmetic and copies ran while one was open for 9% -> 9% of each run, Pallas kernels for 0% -> 0%
where the time goes in v1:
time: 1890 us; the launch traced here: 1870 us
  waiting for transfers between devices  696 us (37%)
  local copies, waits for them, and re-layouts  383 us (20%)
  matrix products  311 us (16%)
  blocking collectives  233 us (12%)
  other arithmetic  176 us (9%)
  loops' own time  34.4 us (2%)
  between operations  20.6 us (1%)
    dynamic_update_slice x10, local copies, waits for them, and re-layouts, scan_ssd(): lax.scan(jax.checkpoint(block_step), initial, sliced)  142 us
    psum x1, waiting for transfers between devices, on_device(): lax.psum(split_sums[0].astype(jnp.bfloat16), 'ctx').astype(jnp.float32)  138 us
    unnamed x10, waiting for transfers between devices  134 us
    all_gather x1, waiting for transfers between devices, on_device(): lax.all_gather(in_matrix, 'fsdp', axis=0, tiled=True)  124 us
    all_gather x1, blocking collectives, on_device(): g_piece = lax.all_gather(input_gain, 'fsdp', axis=0, tiled=True)  103 us
    dot_general x6, matrix products, block_step(): y_diag = jnp.einsum('hts,shp->thp', mixing, xblock, precision=precise)  100 us
    unnamed x150, local copies, waits for them, and re-layouts  94.1 us
    reduce_scatter x1, waiting for transfers between devices, on_device(): lax.psum_scatter(d_out_matrix.astype(jnp.bfloat16), 'fsdp', scatter_dimen...  74.1 us
  transfers between devices with their start and end apart: 14, of which 8 were waited for; matrix products, arithmetic and copies ran while one was open for 9% of the time, Pallas kernels for 0%

profile of v1, /device:TPU:0, one launch (start us, length us, event | category | flops | bytes accessed | tf_op | source)
XLA Modules:
  0.0 1866.0 jit_solution(9849466214441494460)
XLA Ops:
  7.7 56.6 %collective-permute-done.1 = bf16[384,6448]{0,1:T(8,128)(2,1)} collective-permute-done((bf16[384,6448]{0,1:T(8,128)(2,1)}, bf16[384,6448]{0,1:T(8,128)(2,1)}, u32[]{:S(2)}, u32[]{:S(2)}) %collective-permute-start.1) | collective-permute-done | bytes 4952096 | tf_op jit(solution)/shard_map/ppermute | solution.py:182
  71.7 102.8 %all-gather.2 = bf16[4,1,384]{2,1,0:T(2,128)(2,1)S(1)} all-gather(bf16[1,1,384]{2,1,0:T(2,128)(2,1)S(1)} %reshape.543), channel_id=1, replica_groups=mesh['fsdp'=4,'ctx'=8] {'fsdp'}, dimensions={0}, use_global_device_ids=true | all-gather | bytes 3840 | tf_op jit(solution)/shard_map/all_gather | solution.py:187
  180.7 8.6 all-reduce.24
  189.3 5.4 all-gather.3
  202.6 5.4 constant_dynamic-update-slice_fusion.7
  240.3 17.5 fusion.93
  271.1 8.2 fusion.98
  279.3 6.2 slice.212
  287.4 6.6 copy.271
  294.0 8.2 reshape.509
  302.2 6.4 copy.274
  308.6 209.4 %while.80 = (s32[]{:T(128)}, f32[48,64,128]{2,1,0:T(8,128)S(1)}, s32[]{:T(128)}, f32[48]{0:T(128)S(1)}, f32[2,256,48,64]{1,0,3,2:T(2,128)}, /*index=5*/f32[2,256...) while((s32[]{:T(128)}, f32[48,64,128]{2,1,0:T(8,128)S(1)}, ...), condition=%wide.region_4.5_spmd.clone, body=%wide.region_1.4_spmd.clone.sunk | while | flops 4951254016 | bytes 38503760 | solution.py:119
  311.8 16.5 fusion.245
  340.2 63.5 %dynamic_update_slice.95 = f32[2,256,48,64]{1,0,3,2:T(2,128)} dynamic-update-slice(f32[2,256,48,64]{1,0,3,2:T(2,128)} %get-tuple-element.1638, f32[1,256,48,64]{1,0,3,2:T(1,128)} %copy.397, s32[]{:T(128)} %get-tuple-element.1634, s32[]{:T(128)} %constant.217.clone.1..sunk.1, s32[]{:T(128)} %constant.217.clone.1..sunk.1, s32[]{:T(128)} %constant.217.clone.1..sunk.1) | dynamic-update-slice | bytes 6291460 | tf_op jit(solution)/shard_map/jvp()/while/body/jit(dynamic_update_index_in_dim)/dynamic_update_slice | solution.py:119
  416.4 16.5 fusion.245
  444.7 63.5 %dynamic_update_slice.95 = f32[2,256,48,64]{1,0,3,2:T(2,128)} dynamic-update-slice(f32[2,256,48,64]{1,0,3,2:T(2,128)} %get-tuple-element.1638, f32[1,256,48,64]{1,0,3,2:T(1,128)} %copy.397, s32[]{:T(128)} %get-tuple-element.1634, s32[]{:T(128)} %constant.217.clone.1..sunk.1, s32[]{:T(128)} %constant.217.clone.1..sunk.1, s32[]{:T(128)} %constant.217.clone.1..sunk.1) | dynamic-update-slice | bytes 6291460 | tf_op jit(solution)/shard_map/jvp()/while/body/jit(dynamic_update_index_in_dim)/dynamic_update_slice | solution.py:119
  528.8 18.9 %all-gather.4 = bf16[8,1,48]{2,1,0:T(2,128)(2,1)S(1)} all-gather(bf16[1,1,48]{2,1,0:T(2,128)(2,1)S(1)} %bitcast.511), channel_id=1, replica_groups=mesh['fsdp'=4,'ctx'=8] {'ctx'}, dimensions={0}, use_global_device_ids=true | all-gather | bytes 864 | tf_op jit(solution)/shard_map/all_gather | solution.py:27
  547.7 9.0 reshape.512
  556.7 61.0 %all-gather.15.cloned.1.call-done = bf16[384,64,128]{2,1,0:T(8,128)(2,1)} async-done(((bf16[48,64,128]{2,1,0:T(8,128)(2,1)}), bf16[384,64,128]{2,1,0:T(8,128)(2,1)}) %all-gather.15.cloned.1.call-update) | async-done | bytes 6291472 | tf_op jit(solution)/shard_map/all_gather | solution.py:27
  617.9 13.1 multiply_add_fusion.4
  631.0 6.6 copy.278
  637.6 6.8 multiply_reduce_fusion.13
  644.4 37.3 %all-gather.11.cloned.1.call-done = bf16[3072,1536]{1,0:T(8,128)(2,1)} async-done(((bf16[768,1536]{1,0:T(8,128)(2,1)}), bf16[3072,1536]{1,0:T(8,128)(2,1)}) %all-gather.11.cloned.1.call-update) | async-done | bytes 9437200 | tf_op jit(solution)/shard_map/all_gather | solution.py:197
  681.7 12.6 multiply_reduce_fusion.9
  694.4 11.1 multiply_reduce_fusion.10
  705.5 6.6 copy.280
  712.1 8.2 fusion.131
  721.1 10.1 reshape.581
  731.3 11.0 copy.286
  742.3 6.4 multiply_reduce_fusion.11
  748.7 70.8 %all-gather.17.cloned.1.call-done = bf16[384,64,128]{2,1,0:T(8,128)(2,1)} async-done(((bf16[48,64,128]{2,1,0:T(8,128)(2,1)}), bf16[384,64,128]{2,1,0:T(8,128)(2,1)}) %all-gather.17.cloned.1.call-update) | async-done | bytes 6291472 | tf_op jit(solution)/shard_map/all_gather | solution.py:47
  819.5 24.0 %while.81 = (s32[]{:T(128)}, f32[48,64,128]{2,1,0:T(8,128)}, s32[]{:T(128)}, bf16[8,48]{1,0:T(8,128)(2,1)S(1)}, bf16[8,48,64,128]{3,2,1,0:T(8,128)(2,1)}, /*index=5*/s32[]{:T(128)}, s32[]{:T(128)}, s32[]{:T(128)}, s32[]{:T(128)}) while((s32[]{:T(128)}, f32[48,64,128]{2,1,0:T(8,128)}, s32[]{:T(128)}, ...), condition=%wide.region_10.11_spmd.clone, body=%wide.region_9.10_spmd.clone.sunk | while | flops 1966136 | bytes 3932807 | solution.py:63
  852.5 247.5 %while.82 = (s32[]{:T(128)}, f32[48,64,128]{2,1,0:T(8,128)}, f32[48]{0:T(128)}, f32[2,256,48,64]{1,3,2,0:T(8,128)}, f32[2,256,128]{2,1,0:T(8,128)}, /*index=5*/f...) while((s32[]{:T(128)}, f32[48,64,128]{2,1,0:T(8,128)}, ...), condition=%wide.region_26.27_spmd.clone, body=%wide.region_13.26_spmd.clone.sunk | while | flops 11239392256 | bytes 115198616 | solution.py:119
  888.6 6.7 multiply_reduce_fusion.21
  912.2 21.5 %fusion.269 = (f32[48,256]{1,0:T(8,128)S(1)}, f32[48,256]{1,0:T(8,128)S(1)}, f32[48,256]{1,0:T(8,128)}, f32[256,256]{1,0:T(8,128)}) fusion(f32[48,256]{1,0:T(8,128)S(1)} %bitcast.483, f32[256,256]{1,0:T(8,128)S(1)} %fusion.267, f32[48,256]{1,0:T(8,128)} %get-tuple-element.1594, pred[256,256]{1,0:T(8,128)(4,1)S(1)} %fusion.268, ...), kind=kOutput, calls=%fused_computation.72.clone.1 | convolution fusion | flops 2456711168 | bytes 7127040 | tf_op jit(solution)/shard_map/transpose(jvp())/while/body/eval_jaxpr/checkpoint/hts,shp->thp/dot_general | solution.py:82
  947.4 6.4 fusion.274
  955.8 6.5 fusion.272
  963.8 12.2 bitcast_dynamic-update-slice_fusion.7
  998.5 6.7 multiply_reduce_fusion.21
  1022.2 21.5 %fusion.269 = (f32[48,256]{1,0:T(8,128)S(1)}, f32[48,256]{1,0:T(8,128)S(1)}, f32[48,256]{1,0:T(8,128)}, f32[256,256]{1,0:T(8,128)}) fusion(f32[48,256]{1,0:T(8,128)S(1)} %bitcast.483, f32[256,256]{1,0:T(8,128)S(1)} %fusion.267, f32[48,256]{1,0:T(8,128)} %get-tuple-element.1594, pred[256,256]{1,0:T(8,128)(4,1)S(1)} %fusion.268, ...), kind=kOutput, calls=%fused_computation.72.clone.1 | convolution fusion | flops 2456711168 | bytes 7127040 | tf_op jit(solution)/shard_map/transpose(jvp())/while/body/eval_jaxpr/checkpoint/hts,shp->thp/dot_general | solution.py:82
  1057.3 6.4 fusion.274
  1065.8 6.5 fusion.272
  1073.7 12.2 bitcast_dynamic-update-slice_fusion.7
  1100.0 12.7 fusion.137
  1112.6 11.4 copy.299
  1124.0 10.8 reshape.582
  1134.8 6.0 multiply_add_fusion.3
  1140.9 10.7 multiply_reduce_fusion.8
  1151.6 8.1 broadcast_multiply_fusion
  1159.8 8.0 fusion.171
  1178.0 16.4 convolution_convert_fusion
  1194.5 24.2 %copy.300 = bf16[1536,6448]{1,0:T(8,128)(2,1)} copy(bf16[1536,6448]{0,1:T(8,128)(2,1)} %convolution_convert_fusion) | data formatting | bytes 39616512
  1220.1 11.2 convolution_convert_fusion.1
  1233.7 133.1 %reduce-scatter.10.cloned.1.call-done = bf16[384,6448]{1,0:T(8,128)(2,1)} async-done(((bf16[1536,6448]{1,0:T(8,128)(2,1)}), bf16[384,6448]{1,0:T(8,128)(2,1)}) %reduce-scatter.10.cloned.1.call-update) | async-done | bytes 4952080
  1366.8 7.6 copy.301
  1374.4 74.1 %reduce-scatter.8.cloned.1.call-done = bf16[768,1536]{1,0:T(8,128)(2,1)} async-done(((bf16[3072,1536]{1,0:T(8,128)(2,1)}), bf16[768,1536]{1,0:T(8,128)(2,1)}) %reduce-scatter.8.cloned.1.call-update) | async-done | bytes 2359312 | tf_op jit(solution)/shard_map/reduce_scatter | solution.py:298
  1450.7 124.2 %all-gather.13.cloned.1.call-done = bf16[1536,6448]{0,1:T(8,128)(2,1)} async-done(((bf16[384,6448]{0,1:T(8,128)(2,1)}), bf16[1536,6448]{0,1:T(8,128)(2,1)}) %all-gather.13.cloned.1.call-update) | async-done | bytes 19808272 | tf_op jit(solution)/shard_map/all_gather | solution.py:286
  1574.9 19.6 %fusion.140 = f32[512,1536]{1,0:T(8,128)S(1)} fusion(bf16[1536,6448]{0,1:T(8,128)(2,1)} %all-gather.13.cloned.1.call-done, bf16[512,48]{1,0:T(8,128)(2,1)S(1)} %copy-done.49, bf16[3,3328]{1,0:T(4,128)(2,1)S(1)} %fusion.152, bf16[509,3328]{1,0:T(8,128)(2,1)} %copy-done.19, bf16[512,3072]{1,0:T(8,128)(2,1)} %get-tuple-element.1248), kind=kOutput, calls=%fused_computation.224 | convolution fusion | flops 10168238080 | bytes 29556736 | tf_op jit(solution)/shard_map/dot_general | solution.py:284
  1594.5 13.6 multiply_reduce_fusion.15
  1609.4 43.5 %all-reduce.20 = (f32[48]{0:T(128)S(1)}, f32[48]{0:T(128)S(1)}, f32[48]{0:T(128)S(1)}, f32[2]{0:T(128)S(1)}) all-reduce(f32[48]{0:T(128)S(1)} %copy-done.79, f32[48]{0:T(128)S(1)} %fusion.162, f32[48]{0:T(128)S(1)} %reduce_sum.376, f32[2]{0:T(128)S(1)} %pad_maximum_fusion.3), channel_id=1, replica_groups=mesh['fsdp'=4,'ctx'=8] {'fsdp','ctx'}, use_global_device_ids=true, to_apply=%region_42.43 | all-reduce | flops 146 | bytes 1168 | tf_op jit(solution)/shard_map/psum | solution.py:323
  1654.7 11.1 all-reduce.23
  1671.6 37.3 %all-reduce.21 = (bf16[832,4]{0,1:T(4,128)(2,1)S(1)}, bf16[832]{0:T(1024)(128)(2,1)S(1)}, bf16[768]{0:T(1024)(128)(2,1)S(1)}, bf16[384]{0:T(512)(128)(2,1)S(1)}) all-reduce(bf16[832,4]{0,1:T(4,128)(2,1)S(1)} %copy.303, bf16[832]{0:T(1024)(128)(2,1)S(1)} %dynamic-slice.5, ...), channel_id=1, replica_groups=mesh['fsdp'=4,'ctx'=8] {'ctx'}, use_global_device_ids=true, to_apply=%region_37.38 | all-reduce | flops 5312 | bytes 21248 | tf_op jit(solution)/shard_map/psum | solution.py:317
  1711.2 137.6 %all-reduce.27.cloned.1.call-done = (bf16[384,6448]{0,1:T(8,128)(2,1)}, bf16[768,1536]{1,0:T(8,128)(2,1)}) async-done(((bf16[384,6448]{0,1:T(8,128)(2,1)}, bf16[768,1536]{1,0:T(8,128)(2,1)}), (bf16[384,6448]{0,1:T(8,128)(2,1)}, bf16[768,1536]{1,0:T(8,128)(2,1)})) %all-reduce.27.cloned.1.call-update) | async-done | bytes 7311376 | tf_op jit(solution)/shard_map/psum | solution.py:315
  1848.8 7.1 convert_element_type.263
  (509 shorter events, 294.7 us)
Async XLA Ops:
  7.2 610.5 %all-gather.15.cloned.1.call-start = ((), (), s32[]{:S(2)}) async-start(), calls=%async_computation.6 | async-start | bytes 7077888 | tf_op jit(solution)/shard_map/all_gather | solution.py:27
  7.2 57.1 %collective-permute-start.1 = (bf16[384,6448]{0,1:T(8,128)(2,1)}, bf16[384,6448]{0,1:T(8,128)(2,1)}, u32[]{:S(2)}, u32[]{:S(2)}) collective-permute-start(bf16[384,6448]{0,1:T(8,128)(2,1)} %param.23), channel_id=1, source_target_pairs={{0,8},{8,16},{16,24},{24,0},{1,9},{9,17},{17,25},{25,1},{2,10},{10... | collective-permute-start | bytes 14856200 | tf_op jit(solution)/shard_map/ppermute | solution.py:182
  64.3 138.3 %collective-permute-start.2 = (bf16[384,6448]{0,1:T(8,128)(2,1)}, bf16[384,6448]{0,1:T(8,128)(2,1)}, u32[]{:S(2)}, u32[]{:S(2)}) collective-permute-start(bf16[384,6448]{0,1:T(8,128)(2,1)} %collective-permute-done.1), channel_id=1, source_target_pairs={{0,8},{8,16},{16,24},{24,0},{1,9},{9,17},{17,25},{25,1},{2,10},{10... | collective-permute-start | bytes 14856200 | tf_op jit(solution)/shard_map/ppermute | solution.py:182
  64.3 151.9 %collective-permute-start.3 = (bf16[384,6448]{0,1:T(8,128)(2,1)}, bf16[384,6448]{0,1:T(8,128)(2,1)}, u32[]{:S(2)}, u32[]{:S(2)}) collective-permute-start(bf16[384,6448]{0,1:T(8,128)(2,1)} %param.23), channel_id=1, source_target_pairs={{0,24},{8,0},{16,8},{24,16},{1,25},{9,1},{17,9},{25,17},{2,26},{10... | collective-permute-start | bytes 14856200 | tf_op jit(solution)/shard_map/ppermute | solution.py:184
  66.8 131.9 %collective-permute-start = (s32[3]{0:T(128)S(1)}, s32[3]{0:T(128)S(1)}, u32[]{:S(2)}, u32[]{:S(2)}) collective-permute-start(s32[3]{0:T(128)S(1)} %slice_bitcast_fusion), channel_id=1, source_target_pairs={{0,1},{1,2},{2,3},{3,4},{4,5},{5,6},{6,7},{8,9},{9,10},{10,11},{11... | collective-permute-start | bytes 44 | tf_op jit(solution)/shard_map/ppermute | solution.py:21
  174.6 65.7 %copy-start.65 = (f32[1536]{0:T(1024)}, f32[1536]{0:T(1024)S(1)}, u32[]{:S(2)}) copy-start(f32[1536]{0:T(1024)S(1)} %reshape.551) | copy-start | bytes 18436
  194.8 67.7 %copy-start.75 = (f32[48]{0:T(128)}, f32[48]{0:T(128)S(1)}, u32[]{:S(2)}) copy-start(f32[48]{0:T(128)S(1)} %convert_element_type.241) | copy-start | bytes 580
  196.8 74.2 %copy-start.40 = (f32[3328]{0:T(1024)}, f32[3328]{0:T(1024)S(1)}, u32[]{:S(2)}) copy-start(f32[3328]{0:T(1024)S(1)} %get-tuple-element.1104) | copy-start | bytes 39940
  196.8 74.2 %copy-start.42 = (f32[3328]{0:T(1024)}, f32[3328]{0:T(1024)S(1)}, u32[]{:S(2)}) copy-start(f32[3328]{0:T(1024)S(1)} %get-tuple-element.1105) | copy-start | bytes 39940
  196.9 74.2 %copy-start.44 = (f32[3328]{0:T(1024)}, f32[3328]{0:T(1024)S(1)}, u32[]{:S(2)}) copy-start(f32[3328]{0:T(1024)S(1)} %get-tuple-element.1106) | copy-start | bytes 39940
  196.9 74.2 %copy-start.46 = (f32[3328]{0:T(1024)}, f32[3328]{0:T(1024)S(1)}, u32[]{:S(2)}) copy-start(f32[3328]{0:T(1024)S(1)} %get-tuple-element.1107) | copy-start | bytes 39940
  198.7 63.8 %copy-start.77 = (f32[48]{0:T(128)}, f32[48]{0:T(128)S(1)}, u32[]{:S(2)}) copy-start(f32[48]{0:T(128)S(1)} %convert_exponential_fusion) | copy-start | bytes 580
  198.7 41.6 %copy-start.72 = (f32[512]{0:T(512)}, f32[512]{0:T(512)S(1)}, u32[]{:S(2)}) copy-start(f32[512]{0:T(512)S(1)} %add_rsqrt_fusion) | copy-start | bytes 6148
  202.6 68.5 %copy-start.59 = (f32[512]{0:T(512)}, f32[512]{0:T(512)S(1)}, u32[]{:S(2)}) copy-start(f32[512]{0:T(512)S(1)} %get-tuple-element.1259) | copy-start | bytes 6148
  202.6 68.5 %copy-start.61 = (f32[512]{0:T(512)}, f32[512]{0:T(512)S(1)}, u32[]{:S(2)}) copy-start(f32[512]{0:T(512)S(1)} %get-tuple-element.1260) | copy-start | bytes 6148
  202.6 68.5 %copy-start.63 = (f32[512]{0:T(512)}, f32[512]{0:T(512)S(1)}, u32[]{:S(2)}) copy-start(f32[512]{0:T(512)S(1)} %get-tuple-element.1261) | copy-start | bytes 6148
  258.7 9.7 collective-permute-start.4
  308.6 212.6 %copy-start.82 = (bf16[48]{0:T(256)(128)(2,1)S(1)}, bf16[48]{0:T(256)(128)(2,1)}, u32[]{:S(2)}) copy-start(bf16[48]{0:T(256)(128)(2,1)} %get-tuple-element.1208) | copy-start | bytes 292
  308.6 212.6 %copy-start.80 = (bf16[768]{0:T(1024)(128)(2,1)S(1)}, bf16[768]{0:T(1024)(128)(2,1)}, u32[]{:S(2)}) copy-start(bf16[768]{0:T(1024)(128)(2,1)} %param.30) | copy-start | bytes 4612
  518.1 38.6 %copy-start.50 = (s32[2,256]{1,0:T(2,128)}, s32[2,256]{1,0:T(2,128)S(1)}, u32[]{:S(2)}) copy-start(s32[2,256]{1,0:T(2,128)S(1)} %get-tuple-element.1824) | copy-start | bytes 6148
  519.1 162.6 %all-gather.11.cloned.1.call-start = ((), (), s32[]{:S(2)}) async-start(), calls=%async_computation.3 | async-start | bytes 11796480 | tf_op jit(solution)/shard_map/all_gather | solution.py:197
  519.9 299.6 %all-gather.17.cloned.1.call-start = ((), (), s32[]{:S(2)}) async-start(), calls=%async_computation.7 | async-start | bytes 7077888 | tf_op jit(solution)/shard_map/all_gather | solution.py:47
  526.4 168.0 %copy-start.55 = (f32[4,1,768]{2,1,0:T(1,128)}, f32[4,1,768]{2,1,0:T(1,128)S(1)}, u32[]{:S(2)}) copy-start(f32[4,1,768]{2,1,0:T(1,128)S(1)} %convert_element_type.281) | copy-start | bytes 36868
  556.7 155.4 %copy-start.24 = (f32[512,48]{0,1:T(8,128)}, f32[512,48]{0,1:T(8,128)S(1)}, u32[]{:S(2)}) copy-start(f32[512,48]{0,1:T(8,128)S(1)} %exponential_multiply_fusion.4) | copy-start | bytes 294916
  617.9 225.6 %copy-start.2 = (f32[48,64,128]{2,1,0:T(8,128)}, f32[48,64,128]{2,1,0:T(8,128)S(1)}, u32[]{:S(2)}) copy-start(f32[48,64,128]{2,1,0:T(8,128)S(1)} %get-tuple-element.688) | copy-start | bytes 4718596
  637.6 44.1 %copy-start.27 = (bf16[1,512,1536]{2,1,0:T(8,128)(2,1)S(1)}, bf16[1,512,1536]{2,1,0:T(8,128)(2,1)}, u32[]{:S(2)}) copy-start(bf16[1,512,1536]{2,1,0:T(8,128)(2,1)} %param.22) | copy-start | bytes 4718596
  644.4 49.9 %copy-start.70 = (f32[512]{0:T(512)}, f32[512]{0:T(512)S(1)}, u32[]{:S(2)}) copy-start(f32[512]{0:T(512)S(1)} %fusion.158) | copy-start | bytes 6148
  720.3 646.5 %reduce-scatter.10.cloned.1.call-start = ((), (), s32[]{:S(2)}) async-start(), calls=%async_computation.8 | async-start | bytes 25067520
  880.1 32.1 %copy-start.8 = (f32[256,48]{0,1:T(8,128)}, f32[256,48]{0,1:T(8,128)S(1)}, u32[]{:S(2)}) copy-start(f32[256,48]{0,1:T(8,128)S(1)} %get-tuple-element.1590) | copy-start | bytes 147460 | tf_op jit(solution)/shard_map/transpose(jvp())/while
  911.3 22.4 %copy-start.12 = (f32[256,256]{1,0:T(8,128)}, f32[256,256]{1,0:T(8,128)S(1)}, u32[]{:S(2)}) copy-start(f32[256,256]{1,0:T(8,128)S(1)} %fusion.267) | copy-start | bytes 786436 | tf_op jit(solution)/shard_map/transpose(jvp())/while
  912.1 21.5 %copy-start.25 = (pred[256,256]{1,0:T(8,128)(4,1)}, pred[256,256]{1,0:T(8,128)(4,1)S(1)}, u32[]{:S(2)}) copy-start(pred[256,256]{1,0:T(8,128)(4,1)S(1)} %fusion.268) | copy-start | bytes 196612 | tf_op jit(solution)/shard_map/transpose(jvp())/while
  912.2 21.5 %copy-start.18 = (f32[1,256,48]{1,2,0:T(8,128)S(1)}, f32[1,256,48]{1,2,0:T(8,128)}, u32[]{:S(2)}) copy-start(f32[1,256,48]{1,2,0:T(8,128)} %copy.405) | copy-start | bytes 147460 | tf_op jit(solution)/shard_map/transpose(jvp())/while
  912.2 21.5 %copy-start.22 = (f32[1,48]{0,1:T(8,128)S(1)}, f32[1,48]{0,1:T(8,128)}, u32[]{:S(2)}) copy-start(f32[1,48]{0,1:T(8,128)} %copy.406) | copy-start | bytes 580 | tf_op jit(solution)/shard_map/transpose(jvp())/while
  912.2 21.5 %copy-start.35 = (f32[48,2]{0,1:T(2,128)S(1)}, f32[48,2]{0,1:T(2,128)}, u32[]{:S(2)}) copy-start(f32[48,2]{0,1:T(2,128)} %copy-done.34) | copy-start | bytes 1156 | tf_op jit(solution)/shard_map/transpose(jvp())/while
  912.2 21.5 %copy-start.36 = (f32[256]{0:T(256)S(1)}, f32[256]{0:T(256)}, u32[]{:S(2)}) copy-start(f32[256]{0:T(256)} %get-tuple-element.1602) | copy-start | bytes 3076 | tf_op jit(solution)/shard_map/transpose(jvp())/while
  912.2 21.5 %copy-start.39 = (f32[48]{0:T(128)S(1)}, f32[48]{0:T(128)}, u32[]{:S(2)}) copy-start(f32[48]{0:T(128)} %copy-done.38) | copy-start | bytes 580 | tf_op jit(solution)/shard_map/transpose(jvp())/while
  912.2 21.5 %copy-start.52 = (f32[256]{0:T(256)S(1)}, f32[256]{0:T(256)}, u32[]{:S(2)}) copy-start(f32[256]{0:T(256)} %get-tuple-element.1607) | copy-start | bytes 3076 | tf_op jit(solution)/shard_map/transpose(jvp())/while
  943.1 20.6 %copy-start.3 = (f32[256,48,64]{0,2,1:T(8,128)S(1)}, f32[256,48,64]{0,2,1:T(8,128)}, u32[]{:S(2)}) copy-start(f32[256,48,64]{0,2,1:T(8,128)} %get-tuple-element.1611) | copy-start | bytes 9437188 | tf_op jit(solution)/shard_map/transpose(jvp())/while
  943.1 20.6 %copy-start.9 = (f32[256,48]{0,1:T(8,128)S(1)}, f32[256,48]{0,1:T(8,128)}, u32[]{:S(2)}) copy-start(f32[256,48]{0,1:T(8,128)} %copy-done.8) | copy-start | bytes 147460 | tf_op jit(solution)/shard_map/transpose(jvp())/while
  943.1 20.6 %copy-start.13 = (f32[256,256]{1,0:T(8,128)S(1)}, f32[256,256]{1,0:T(8,128)}, u32[]{:S(2)}) copy-start(f32[256,256]{1,0:T(8,128)} %copy-done.12) | copy-start | bytes 786436 | tf_op jit(solution)/shard_map/transpose(jvp())/while
  989.4 32.7 %copy-start.8 = (f32[256,48]{0,1:T(8,128)}, f32[256,48]{0,1:T(8,128)S(1)}, u32[]{:S(2)}) copy-start(f32[256,48]{0,1:T(8,128)S(1)} %get-tuple-element.1590) | copy-start | bytes 147460 | tf_op jit(solution)/shard_map/transpose(jvp())/while
  1021.2 22.4 %copy-start.12 = (f32[256,256]{1,0:T(8,128)}, f32[256,256]{1,0:T(8,128)S(1)}, u32[]{:S(2)}) copy-start(f32[256,256]{1,0:T(8,128)S(1)} %fusion.267) | copy-start | bytes 786436 | tf_op jit(solution)/shard_map/transpose(jvp())/while
  1022.1 21.5 %copy-start.25 = (pred[256,256]{1,0:T(8,128)(4,1)}, pred[256,256]{1,0:T(8,128)(4,1)S(1)}, u32[]{:S(2)}) copy-start(pred[256,256]{1,0:T(8,128)(4,1)S(1)} %fusion.268) | copy-start | bytes 196612 | tf_op jit(solution)/shard_map/transpose(jvp())/while
  1022.1 21.5 %copy-start.18 = (f32[1,256,48]{1,2,0:T(8,128)S(1)}, f32[1,256,48]{1,2,0:T(8,128)}, u32[]{:S(2)}) copy-start(f32[1,256,48]{1,2,0:T(8,128)} %copy.405) | copy-start | bytes 147460 | tf_op jit(solution)/shard_map/transpose(jvp())/while
  1022.1 21.5 %copy-start.22 = (f32[1,48]{0,1:T(8,128)S(1)}, f32[1,48]{0,1:T(8,128)}, u32[]{:S(2)}) copy-start(f32[1,48]{0,1:T(8,128)} %copy.406) | copy-start | bytes 580 | tf_op jit(solution)/shard_map/transpose(jvp())/while
  1022.1 21.5 %copy-start.35 = (f32[48,2]{0,1:T(2,128)S(1)}, f32[48,2]{0,1:T(2,128)}, u32[]{:S(2)}) copy-start(f32[48,2]{0,1:T(2,128)} %copy-done.34) | copy-start | bytes 1156 | tf_op jit(solution)/shard_map/transpose(jvp())/while
  1022.2 21.5 %copy-start.36 = (f32[256]{0:T(256)S(1)}, f32[256]{0:T(256)}, u32[]{:S(2)}) copy-start(f32[256]{0:T(256)} %get-tuple-element.1602) | copy-start | bytes 3076 | tf_op jit(solution)/shard_map/transpose(jvp())/while
  1022.2 21.5 %copy-start.39 = (f32[48]{0:T(128)S(1)}, f32[48]{0:T(128)}, u32[]{:S(2)}) copy-start(f32[48]{0:T(128)} %copy-done.38) | copy-start | bytes 580 | tf_op jit(solution)/shard_map/transpose(jvp())/while
  1022.2 21.5 %copy-start.52 = (f32[256]{0:T(256)S(1)}, f32[256]{0:T(256)}, u32[]{:S(2)}) copy-start(f32[256]{0:T(256)} %get-tuple-element.1607) | copy-start | bytes 3076 | tf_op jit(solution)/shard_map/transpose(jvp())/while
  1053.0 20.6 %copy-start.3 = (f32[256,48,64]{0,2,1:T(8,128)S(1)}, f32[256,48,64]{0,2,1:T(8,128)}, u32[]{:S(2)}) copy-start(f32[256,48,64]{0,2,1:T(8,128)} %get-tuple-element.1611) | copy-start | bytes 9437188 | tf_op jit(solution)/shard_map/transpose(jvp())/while
  1053.0 20.6 %copy-start.9 = (f32[256,48]{0,1:T(8,128)S(1)}, f32[256,48]{0,1:T(8,128)}, u32[]{:S(2)}) copy-start(f32[256,48]{0,1:T(8,128)} %copy-done.8) | copy-start | bytes 147460 | tf_op jit(solution)/shard_map/transpose(jvp())/while
  1053.0 20.6 %copy-start.13 = (f32[256,256]{1,0:T(8,128)S(1)}, f32[256,256]{1,0:T(8,128)}, u32[]{:S(2)}) copy-start(f32[256,256]{1,0:T(8,128)} %copy-done.12) | copy-start | bytes 786436 | tf_op jit(solution)/shard_map/transpose(jvp())/while
  1053.0 20.6 %copy-start.17 = (f32[256,48]{0,1:T(8,128)S(1)}, f32[256,48]{0,1:T(8,128)}, u32[]{:S(2)}) copy-start(f32[256,48]{0,1:T(8,128)} %get-tuple-element.1612) | copy-start | bytes 147460 | tf_op jit(solution)/shard_map/transpose(jvp())/while
  1168.4 7.9 collective-permute-start.5
  1218.7 229.8 %reduce-scatter.8.cloned.1.call-start = ((), (), s32[]{:S(2)}) async-start(), calls=%async_computation.5 | async-start | bytes 11796480 | tf_op jit(solution)/shard_map/reduce_scatter | solution.py:298
  1231.3 343.6 %all-gather.13.cloned.1.call-start = ((), (), s32[]{:S(2)}) async-start(), calls=%async_computation.4 | async-start | bytes 24760320 | tf_op jit(solution)/shard_map/all_gather | solution.py:286
  1231.8 438.7 %reduce-scatter.12.cloned.1.call-start = ((), (), s32[]{:S(2)}) async-start(), calls=%async_computation.9 | async-start | bytes 1064960
  1233.3 217.1 %copy-start.57 = (f32[3072]{0:T(1024)S(1)}, f32[3072]{0:T(1024)}, u32[]{:S(2)}) copy-start(f32[3072]{0:T(1024)} %get-tuple-element.1211) | copy-start | bytes 36868
  1233.3 217.3 %copy-start.81 = (f32[48]{0:T(128)S(1)}, f32[48]{0:T(128)}, u32[]{:S(2)}) copy-start(f32[48]{0:T(128)} %get-tuple-element.1249) | copy-start | bytes 580
  1233.3 217.3 %copy-start.84 = (bf16[48]{0:T(256)(128)(2,1)S(1)}, bf16[48]{0:T(256)(128)(2,1)}, u32[]{:S(2)}) copy-start(bf16[48]{0:T(256)(128)(2,1)} %copy-done.83) | copy-start | bytes 292
  1233.4 341.5 %copy-start.49 = (bf16[512,48]{1,0:T(8,128)(2,1)S(1)}, bf16[512,48]{1,0:T(8,128)(2,1)}, u32[]{:S(2)}) copy-start(bf16[512,48]{1,0:T(8,128)(2,1)} %copy-done.48) | copy-start | bytes 147460
  1233.4 615.5 %all-reduce.27.cloned.1.call-start = ((), (), s32[]{:S(2)}) async-start(), calls=%async_computation.10 | async-start | bytes 14622720 | tf_op jit(solution)/shard_map/psum | solution.py:315
  1450.7 143.8 %copy-start.16 = (bf16[1,512,1536]{2,1,0:T(8,128)(2,1)S(1)}, bf16[1,512,1536]{2,1,0:T(8,128)(2,1)}, u32[]{:S(2)}) copy-start(bf16[1,512,1536]{2,1,0:T(8,128)(2,1)} %param.20) | copy-start | bytes 4718596
  1594.5 60.2 %copy-start.74 = (bf16[3072]{0:T(1024)(128)(2,1)S(1)}, bf16[3072]{0:T(1024)(128)(2,1)}, u32[]{:S(2)}) copy-start(bf16[3072]{0:T(1024)(128)(2,1)} %get-tuple-element.1095) | copy-start | bytes 18436
  (69 other events, 678.2 us)
Sparse Core Ops, SparseCore 0:
  519.2 98.4 all-gather.14
  619.3 62.4 all-gather.10
  720.4 99.0 all-gather.16
  1218.8 147.9 reduce-scatter.9
  1370.0 78.4 reduce-scatter.7
  1450.0 124.8 all-gather.12
  1577.6 23.6 reduce-scatter.11
  1605.4 243.4 all-reduce.26
